TPU v7x, 256 devices: a whole 4x4x8 slice. The times are simulated.
256 devices in a mesh: date: 32 (over z, y_lo, core), strip: 8 (over x, y_hi).
Axes of the slice: x: 4, y: 4 (y_hi: 2, y_lo: 2; y = y_hi * 2 + y_lo), z: 8, core: 2. Of those that a mesh axis runs over, the one named last changes fastest.
Arguments:
- acquisitions: bfloat16 [64, 2, 2, 344, 2560], P('date', None, None, None, 'strip'), may hold values from -6 to 6
- shifts: int32 [2, 64, 2, 5, 40], P(None, 'date', None, None, 'strip'), may hold values from -8 to 8, as said below
- fractions: int32 [2, 64, 2, 5, 40], P(None, 'date', None, None, 'strip'), may hold values from 0 to 63
- ref_dates: int32 [2], replicated, may hold values from 0 to 63, as said below
Outputs:
- chip_corr: float32 [2, 64, 2, 5, 40], P(None, 'date', None, None, 'strip')
- coherence: float32 [2, 63, 2, 64, 128], P(None, None, None, 'date', 'strip')
Inputs may be any that keep to these rules, and one draw needn't show every extreme that they name: `shifts`: zero at every chip of date ref_dates[t] in tile t. `ref_dates`: the reference dates of consecutive tiles lie in different blocks of 2 dates.
All inputs are finite; a program needn't handle non-finite values.
Results may differ from a plain program's by a relative error of at most 0.0021.
Values may be sent and summed in bfloat16 or wider, within the bound.
No kernel may reach another device: no remote copies, remote signals or barrier semaphores. Data moves between devices by JAX's collectives and lax.ppermute only.
A program may use at most 64 MiB of HBM per device.

v0:
```python
import jax
import jax.numpy as jnp
from jax import lax
from jax.sharding import PartitionSpec as P

TILE_COUNT = 2
CHIP_SIZE = 64
TAP_COUNT = 8
SUBSTEPS = 64
LOOK_AZ = 5
LOOK_RG = 20
MARGIN = 12
epsilon = 1e-06


def padded_2(block, sides, width):
    for axis, dim in sides:
        count = lax.axis_size(axis)
        forward = [(i, i + 1) for i in range(count - 1)]
        backward = [(target, source) for source, target in forward]
        low = lax.ppermute(
            lax.slice_in_dim(block, block.shape[dim] - width, None, axis=dim), axis, forward
        )
        high = lax.ppermute(lax.slice_in_dim(block, 0, width, axis=dim), axis, backward)
        block = jnp.concatenate([low, block, high], axis=dim)
    return block


def spread(value, axis, source):
    kept = jnp.where(lax.axis_index(axis) == source, value, 0).astype(value.dtype)
    return lax.psum(kept, axis)


def sinc_matrix(shift_part, fraction_part):
    window_size = CHIP_SIZE + 2 * MARGIN
    offset = fraction_part.astype(jnp.float32) / SUBSTEPS
    tap_axis = jnp.arange(TAP_COUNT).astype(jnp.float32)
    distance = tap_axis - (TAP_COUNT // 2 - 1) - offset[..., None]
    weights = jnp.sinc(distance) * (0.5 + 0.5 * jnp.cos(jnp.pi * distance / (TAP_COUNT // 2)))
    weights = weights / jnp.sum(weights, axis=-1, keepdims=True)
    out_rows = jnp.arange(CHIP_SIZE, dtype=jnp.int32)[:, None]
    in_rows = jnp.arange(window_size, dtype=jnp.int32)[None, :]
    matrix = jnp.zeros(shift_part.shape + (CHIP_SIZE, window_size), jnp.float32)
    for tap_index in range(TAP_COUNT):
        target = out_rows + shift_part[..., None, None] + (tap_index - TAP_COUNT // 2 + 1 + MARGIN)
        matrix = matrix + jnp.where(
            in_rows == target, weights[..., tap_index][..., None, None], 0.0
        )
    return matrix.astype(jnp.bfloat16)


def correlate(reference_tiles, resampled):
    chips_az = resampled.shape[-2] // CHIP_SIZE
    chips_rg = resampled.shape[-1] // CHIP_SIZE

    def as_chips(values):
        return values.astype(jnp.float32).reshape(
            values.shape[:-2] + (chips_az, CHIP_SIZE, chips_rg, CHIP_SIZE)
        )

    ref_chips = as_chips(reference_tiles)
    sec_chips = as_chips(resampled)
    ref_real = ref_chips[..., 0, :, :, :, :]
    ref_imag = ref_chips[..., 1, :, :, :, :]
    sec_real = sec_chips[..., 0, :, :, :, :]
    sec_imag = sec_chips[..., 1, :, :, :, :]
    cross_real = jnp.sum(ref_real * sec_real + ref_imag * sec_imag, axis=(-3, -1))
    cross_imag = jnp.sum(ref_imag * sec_real - ref_real * sec_imag, axis=(-3, -1))
    ref_power = jnp.sum(ref_real * ref_real + ref_imag * ref_imag, axis=(-3, -1))
    sec_power = jnp.sum(sec_real * sec_real + sec_imag * sec_imag, axis=(-3, -1))
    denominator = jnp.sqrt((ref_power + epsilon) * (sec_power + epsilon))
    return jnp.stack([cross_real / denominator, cross_imag / denominator])


def multilook_pairs(series):
    values = series.astype(jnp.float32)
    earlier = values[:-1]
    second = values[1:]
    early_real = earlier[:, :, 0]
    early_imag = earlier[:, :, 1]
    later_real = second[:, :, 0]
    later_imag = second[:, :, 1]
    cross_real = early_real * later_real + early_imag * later_imag
    cross_imag = early_imag * later_real - early_real * later_imag
    power_early = early_real * early_real + early_imag * early_imag
    power_later = later_real * later_real + later_imag * later_imag

    def box_sum(quantity):
        blocked = quantity.reshape(
            quantity.shape[:2]
            + (quantity.shape[2] // LOOK_AZ, LOOK_AZ, quantity.shape[3] // LOOK_RG, LOOK_RG)
        )
        return jnp.sum(blocked, axis=(3, 5))

    denominator = jnp.sqrt((box_sum(power_early) + epsilon) * (box_sum(power_later) + epsilon))
    return jnp.stack([box_sum(cross_real) / denominator, box_sum(cross_imag) / denominator])


def resample(padded, shift_part, fraction_part):
    window_size = CHIP_SIZE + 2 * MARGIN
    chips_az = shift_part.shape[3]
    chips_rg = shift_part.shape[4]
    pieces = [
        padded[
            :,
            :,
            :,
            chip_row * CHIP_SIZE : chip_row * CHIP_SIZE + window_size,
            chip_col * CHIP_SIZE : chip_col * CHIP_SIZE + window_size,
        ]
        for chip_row in range(chips_az)
        for chip_col in range(chips_rg)
    ]
    windows = jnp.stack(pieces, axis=3).reshape(
        padded.shape[:3] + (chips_az, chips_rg, window_size, window_size)
    )
    azimuth = sinc_matrix(shift_part[0], fraction_part[0])
    across = sinc_matrix(shift_part[1], fraction_part[1])
    partial_rows = jnp.einsum(
        "dtariw,dtcarwv->dtcariv", azimuth, windows, preferred_element_type=jnp.float32
    ).astype(jnp.bfloat16)
    chips_out = jnp.einsum(
        "dtcariv,dtarjv->dtcarij", partial_rows, across, preferred_element_type=jnp.float32
    ).astype(jnp.bfloat16)
    return chips_out.transpose(0, 1, 2, 3, 5, 4, 6).reshape(
        padded.shape[:3] + (chips_az * CHIP_SIZE, chips_rg * CHIP_SIZE)
    )


def per_device(acquisitions, shifts, fractions, ref_dates):
    dates_local = acquisitions.shape[0]
    tile_rows = acquisitions.shape[3] - 2 * MARGIN
    padded = padded_2(acquisitions, (("strip", 4),), MARGIN)
    owners = ref_dates // dates_local
    slots = ref_dates % dates_local
    candidates = [
        lax.dynamic_index_in_dim(acquisitions[:, tile_index], slots[tile_index], 0, keepdims=False)[
            :, MARGIN : MARGIN + tile_rows, :
        ]
        for tile_index in range(TILE_COUNT)
    ]
    reference_tiles = jnp.stack(
        [
            spread(candidates[tile_index], "date", owners[tile_index])
            for tile_index in range(TILE_COUNT)
        ]
    )
    resampled = resample(padded, shifts, fractions)
    chip_corr = correlate(reference_tiles, resampled)
    coherence = multilook_pairs(
        lax.all_to_all(resampled, "date", split_axis=3, concat_axis=0, tiled=True)
    )
    return (chip_corr, coherence)


def solution(mesh):
    return jax.shard_map(
        per_device,
        mesh=mesh,
        in_specs=(
            P("date", None, None, None, "strip"),
            P(None, "date", None, None, "strip"),
            P(None, "date", None, None, "strip"),
            P(),
        ),
        out_specs=(P(None, "date", None, None, "strip"), P(None, None, None, "date", "strip")),
        check_vma=False,
    )
```

profile of v0, /device:TPU:1, one launch (start us, length us, event | category | flops | bytes accessed | tf_op | source)
XLA Modules:
  0.0 462.1 jit_solution(9222938451931565228)
XLA Ops:
  7.2 1.8 fusion.119
  9.0 1.3 collective-permute-start.1
  10.2 6.3 %collective-permute-start = (bf16[2,2,2,344,12]{3,4,2,1,0:T(8,128)(2,1)}, bf16[2,2,2,344,12]{3,4,2,1,0:T(8,128)(2,1)S(1)}, u32[]{:S(2)}, u32[]{:S(2)}) collective-permute-start(bf16[2,2,2,344,12]{3,4,2,1,0:T(8,128)(2,1)} %get-tuple-element.23), channel_id=1, source_target_pairs={{0,1},{1,2},{2,3},{3,4},{4,5},{5,6},{6,7},{8,9},{9,10},{10,11},{11... | collective-permute-start | bytes 198152 | tf_op jit(solution)/shard_map/ppermute | solution.py:21
  20.4 2.7 fusion.118
  23.0 1.5 constant_dynamic-update-slice_fusion.1
  25.9 3.2 fusion.114
  29.1 3.1 broadcast_divide_fusion.1
  42.5 1.2 fusion.104
  43.7 1.1 dynamic-slice_bitcast_fusion.1
  45.0 0.9 dynamic-slice_bitcast_fusion
  48.8 1.5 constant_dynamic-update-slice_fusion
  50.4 1.6 fusion.71
  52.0 0.8 fusion.70
  52.9 0.8 bitcast_dynamic-update-slice_fusion.11
  54.5 0.8 bitcast_dynamic-update-slice_fusion.9
  55.4 1.8 fusion.69
  60.1 1.6 fusion.67
  61.8 0.8 fusion.66
  62.6 0.8 bitcast_dynamic-update-slice_fusion.5
  63.4 0.8 bitcast_dynamic-update-slice_fusion.4
  64.3 0.8 bitcast_dynamic-update-slice_fusion.3
  65.1 1.8 fusion.65
  69.9 1.6 fusion.62
  71.7 7.4 %copy.137 = bf16[2,2,2,25,88,88]{5,4,2,3,1,0:T(8,128)(2,1)} copy(bf16[2,2,2,25,88,88]{4,5,2,1,0,3:T(8,128)(2,1)} %fusion.62) | data formatting | bytes 6195200 | tf_op jit(solution)/shard_map/stack | solution.py:114
  79.4 13.2 %fusion.4.clone.5 = bf16[2,2,2,5,5,64,88]{6,5,2,4,3,1,0:T(8,128)(2,1)S(1)} fusion(bf16[2,2,2,5,5,88,88]{6,5,2,4,3,1,0:T(8,128)(2,1)} %bitcast.220, f32[2,2,5,5]{3,2,1,0:T(8,128)S(1)} %copy-done.26, s32[2,2,5,5,64]{4,3,2,1,0:T(8,128)S(1)} %copy-done.11, f32[2,2,5,5]{3,2,1,0:T(8,128)S(1)} %copy-done.28, ...), kind=kOutput, calls=%fused_computation.3.clone.clone.clone.clone.clone.2 | convolution fusion | flops 212889600 | bytes 5558400 | tf_op jit(solution)/shard_map/dtariw,dtcarwv->dtcariv/dot_general | solution.py:119
  92.7 13.8 %fusion.122 = (f32[2,2,2,5,64,5,64]{4,6,2,5,3,1,0:T(8,128)}, bf16[2,2,2,5,64,5,64]{4,6,2,5,3,1,0:T(8,128)(2,1)}) fusion(f32[2,2,5,5]{3,2,1,0:T(8,128)S(1)} %copy-done.27, s32[2,2,5,5,64]{4,3,2,1,0:T(8,128)S(1)} %copy-done.8, f32[2,2,5,5]{3,2,1,0:T(8,128)S(1)} %copy-done.25, s32[2,2,5,5,64]{4,3,2,1,0:T(8,128)S(1)} %copy-done.7, ...), kind=kOutput, calls=%fused_computation.226 | convolution fusion | flops 159334400 | bytes 7376000 | tf_op jit(solution)/shard_map/dtcariv,dtarjv->dtcarij/dot_general | solution.py:122
  106.5 7.8 %copy.165 = bf16[2,2,2,5,64,5,64]{6,5,2,1,0,4,3:T(8,128)(2,1)} copy(bf16[2,2,2,5,64,5,64]{4,6,2,5,3,1,0:T(8,128)(2,1)} %get-tuple-element.73) | data formatting | bytes 3276800 | tf_op jit(solution)/shard_map/reshape | solution.py:125
  114.3 8.2 %reshape.249 = bf16[2,2,2,320,320]{4,2,1,0,3:T(2,128)(2,1)} reshape(bf16[2,2,2,5,64,5,64]{6,5,2,1,0,4,3:T(8,128)(2,1)} %copy.165) | data formatting | bytes 3276800 | tf_op jit(solution)/shard_map/reshape | solution.py:125
  122.5 11.0 %all-to-all-start = ((bf16[2,2,2,320,320]{4,2,1,0,3:T(2,128)(2,1)}), bf16[2,2,2,320,320]{4,2,1,0,3:T(2,128)(2,1)S(1)}, u32[]{:S(2)}, u32[]{:S(2)}) async-start(bf16[2,2,2,320,320]{4,2,1,0,3:T(2,128)(2,1)} %reshape.249), calls=%async_computation | async-start | bytes 3932160 | tf_op jit(solution)/shard_map/all_to_all | solution.py:151
  134.5 1.6 stack.98
  136.1 1.6 stack.97
  137.7 245.5 %all-reduce.3.cloned.1.call-done = (bf16[1,2,5,64,5,64]{5,4,3,2,1,0:T(8,128)(2,1)}, bf16[1,2,5,64,5,64]{5,4,3,2,1,0:T(8,128)(2,1)}) async-done(((bf16[1,2,5,64,5,64]{5,4,3,2,1,0:T(8,128)(2,1)}, bf16[1,2,5,64,5,64]{5,4,3,2,1,0:T(8,128)(2,1)}), (bf16[1,2,5,64,5,64]{5,4,3,2,1,0:T(8,128)(2,1)}, bf16[1,2,5,64,5,64]{5,4,3,2,1,0:T(8,128)(2,1)})) %all-reduce.3.cloned.1.call-update) | async-done | bytes 819216 | tf_op jit(solution)/shard_map/psum | solution.py:31
  383.2 2.7 maximum_convert_fusion
  386.5 2.8 slice_bitcast_fusion.3
  389.3 2.9 copy.127
  392.2 2.9 copy.148
  395.1 4.9 %add_reduce_fusion.1 = (f32[2,2,5,5]{3,2,1,0:T(8,128)S(1)}, f32[2,2,5,5]{3,2,1,0:T(8,128)S(1)}, f32[2,2,5,5]{3,2,1,0:T(8,128)S(1)}) fusion(f32[2,2,2,5,64,5,64]{4,6,2,5,3,1,0:T(8,128)} %get-tuple-element.72, f32[2,5,64,5,64]{2,4,3,1,0:T(8,128)} %copy.148, f32[2,5,64,5,64]{2,4,3,1,0:T(8,128)} %copy.127), kind=kLoop, calls=%fused_computation.6 | loop fusion | flops 4914900 | bytes 4916400 | tf_op jit(solution)/shard_map/reduce_sum | solution.py:67
  400.9 3.0 copy.156
  403.9 1.3 copy.157
  405.3 9.2 %multiply_add_fusion.2 = (f32[63,2,1,10,320]{4,2,3,1,0:T(1,128)}, f32[63,2,1,10,320]{4,2,3,1,0:T(1,128)}, f32[63,2,1,10,320]{4,2,3,1,0:T(1,128)}, f32[63,2,1,10,320]{4,2,3,1,0:T(1,128)S(1)}) fusion(f32[64,2,2,10,320]{4,2,3,1,0:T(2,128)S(1)} %bitcast.214), kind=kLoop, calls=%fused_computation.35 | loop fusion | flops 4838400 | bytes 12902400 | tf_op jit(solution)/shard_map/add | solution.py:83
  414.5 7.4 %copy.158 = f32[63,2,1,10,320]{0,1,4,3,2:T(2,128)} copy(f32[63,2,1,10,320]{4,2,3,1,0:T(1,128)} %get-tuple-element.16) | data formatting | bytes 3225600 | tf_op jit(solution)/shard_map/add | solution.py:83
  421.9 7.4 %copy.159 = f32[63,2,1,10,320]{0,1,4,3,2:T(2,128)} copy(f32[63,2,1,10,320]{4,2,3,1,0:T(1,128)} %get-tuple-element.17) | data formatting | bytes 3225600 | tf_op jit(solution)/shard_map/add | solution.py:85
  429.3 3.2 reduce_sum.102
  432.5 3.2 reduce_sum.103
  435.7 7.4 %copy.160 = f32[63,2,1,10,320]{0,1,4,3,2:T(2,128)} copy(f32[63,2,1,10,320]{4,2,3,1,0:T(1,128)} %get-tuple-element.18) | data formatting | bytes 3225600 | tf_op jit(solution)/shard_map/add | solution.py:86
  443.1 3.2 reduce_sum.104
  446.3 4.9 %copy.161 = f32[63,2,1,10,320]{0,1,4,3,2:T(2,128)} copy(f32[63,2,1,10,320]{4,2,3,1,0:T(1,128)S(1)} %get-tuple-element.19) | data formatting | bytes 3225600 | tf_op jit(solution)/shard_map/sub | solution.py:84
  451.3 3.2 reduce_sum.105
  (126 shorter events, 23.6 us)
Async XLA Ops:
  7.2 15.9 %copy-start = (bf16[2,2,2,344,320]{3,4,2,1,0:T(8,128)(2,1)S(1)}, bf16[2,2,2,344,320]{3,4,2,1,0:T(8,128)(2,1)}, u32[]{:S(2)}) copy-start(bf16[2,2,2,344,320]{3,4,2,1,0:T(8,128)(2,1)} %param.5) | copy-start | bytes 5283844
  9.0 39.9 %collective-permute-start.1 = (bf16[2,2,2,344,12]{3,4,2,1,0:T(8,128)(2,1)}, bf16[2,2,2,344,12]{3,4,2,1,0:T(8,128)(2,1)}, u32[]{:S(2)}, u32[]{:S(2)}) collective-permute-start(bf16[2,2,2,344,12]{3,4,2,1,0:T(8,128)(2,1)} %get-tuple-element.22), channel_id=1, source_target_pairs={{1,0},{2,1},{3,2},{4,3},{5,4},{6,5},{7,6},{9,8},{10,9},{11,10},{12... | collective-permute-start | bytes 198152 | tf_op jit(solution)/shard_map/ppermute | solution.py:24
  10.2 35.7 %collective-permute-start = (bf16[2,2,2,344,12]{3,4,2,1,0:T(8,128)(2,1)}, bf16[2,2,2,344,12]{3,4,2,1,0:T(8,128)(2,1)S(1)}, u32[]{:S(2)}, u32[]{:S(2)}) collective-permute-start(bf16[2,2,2,344,12]{3,4,2,1,0:T(8,128)(2,1)} %get-tuple-element.23), channel_id=1, source_target_pairs={{0,1},{1,2},{2,3},{3,4},{4,5},{5,6},{6,7},{8,9},{9,10},{10,11},{11... | collective-permute-start | bytes 198152 | tf_op jit(solution)/shard_map/ppermute | solution.py:21
  20.3 5.5 %copy-start.18 = (s32[2,2,2,5,5]{4,2,3,1,0:T(2,128)S(1)}, s32[2,2,2,5,5]{4,2,3,1,0:T(2,128)}, u32[]{:S(2)}) copy-start(s32[2,2,2,5,5]{4,2,3,1,0:T(2,128)} %param.6) | copy-start | bytes 2404
  20.3 5.5 %copy-start.19 = (s32[2,2,2,5,5]{4,2,3,1,0:T(2,128)S(1)}, s32[2,2,2,5,5]{4,2,3,1,0:T(2,128)}, u32[]{:S(2)}) copy-start(s32[2,2,2,5,5]{4,2,3,1,0:T(2,128)} %param.7) | copy-start | bytes 2404
  71.6 7.5 %copy-start.10 = (s32[2,2,5,5,64]{4,3,2,1,0:T(8,128)S(1)}, s32[2,2,5,5,64]{4,3,2,1,0:T(8,128)}, u32[]{:S(2)}) copy-start(s32[2,2,5,5,64]{4,3,2,1,0:T(8,128)} %get-tuple-element.56) | copy-start | bytes 76804
  71.6 7.5 %copy-start.11 = (s32[2,2,5,5,64]{4,3,2,1,0:T(8,128)S(1)}, s32[2,2,5,5,64]{4,3,2,1,0:T(8,128)}, u32[]{:S(2)}) copy-start(s32[2,2,5,5,64]{4,3,2,1,0:T(8,128)} %get-tuple-element.57) | copy-start | bytes 76804
  71.6 7.5 %copy-start.12 = (s32[2,2,5,5,64]{4,3,2,1,0:T(8,128)S(1)}, s32[2,2,5,5,64]{4,3,2,1,0:T(8,128)}, u32[]{:S(2)}) copy-start(s32[2,2,5,5,64]{4,3,2,1,0:T(8,128)} %get-tuple-element.58) | copy-start | bytes 76804
  71.6 7.5 %copy-start.13 = (s32[2,2,5,5,64]{4,3,2,1,0:T(8,128)S(1)}, s32[2,2,5,5,64]{4,3,2,1,0:T(8,128)}, u32[]{:S(2)}) copy-start(s32[2,2,5,5,64]{4,3,2,1,0:T(8,128)} %get-tuple-element.59) | copy-start | bytes 76804
  71.6 7.5 %copy-start.14 = (s32[2,2,5,5,64]{4,3,2,1,0:T(8,128)S(1)}, s32[2,2,5,5,64]{4,3,2,1,0:T(8,128)}, u32[]{:S(2)}) copy-start(s32[2,2,5,5,64]{4,3,2,1,0:T(8,128)} %get-tuple-element.60) | copy-start | bytes 76804
  71.6 7.5 %copy-start.15 = (s32[2,2,5,5,64]{4,3,2,1,0:T(8,128)S(1)}, s32[2,2,5,5,64]{4,3,2,1,0:T(8,128)}, u32[]{:S(2)}) copy-start(s32[2,2,5,5,64]{4,3,2,1,0:T(8,128)} %get-tuple-element.61) | copy-start | bytes 76804
  71.6 7.5 %copy-start.16 = (s32[2,2,5,5,64]{4,3,2,1,0:T(8,128)S(1)}, s32[2,2,5,5,64]{4,3,2,1,0:T(8,128)}, u32[]{:S(2)}) copy-start(s32[2,2,5,5,64]{4,3,2,1,0:T(8,128)} %get-tuple-element.62) | copy-start | bytes 76804
  71.6 7.5 %copy-start.17 = (s32[2,2,5,5,64]{4,3,2,1,0:T(8,128)S(1)}, s32[2,2,5,5,64]{4,3,2,1,0:T(8,128)}, u32[]{:S(2)}) copy-start(s32[2,2,5,5,64]{4,3,2,1,0:T(8,128)} %get-tuple-element.63) | copy-start | bytes 76804
  71.6 7.5 %copy-start.24 = (f32[2,2,5,5]{3,2,1,0:T(8,128)S(1)}, f32[2,2,5,5]{3,2,1,0:T(8,128)}, u32[]{:S(2)}) copy-start(f32[2,2,5,5]{3,2,1,0:T(8,128)} %copy.139) | copy-start | bytes 1204
  71.6 7.5 %copy-start.26 = (f32[2,2,5,5]{3,2,1,0:T(8,128)S(1)}, f32[2,2,5,5]{3,2,1,0:T(8,128)}, u32[]{:S(2)}) copy-start(f32[2,2,5,5]{3,2,1,0:T(8,128)} %copy.146) | copy-start | bytes 1204
  71.6 7.5 %copy-start.28 = (f32[2,2,5,5]{3,2,1,0:T(8,128)S(1)}, f32[2,2,5,5]{3,2,1,0:T(8,128)}, u32[]{:S(2)}) copy-start(f32[2,2,5,5]{3,2,1,0:T(8,128)} %copy.145) | copy-start | bytes 1204
  71.6 7.5 %copy-start.29 = (f32[2,2,5,5]{3,2,1,0:T(8,128)S(1)}, f32[2,2,5,5]{3,2,1,0:T(8,128)}, u32[]{:S(2)}) copy-start(f32[2,2,5,5]{3,2,1,0:T(8,128)} %copy.144) | copy-start | bytes 1204
  71.6 7.5 %copy-start.31 = (f32[2,2,5,5]{3,2,1,0:T(8,128)S(1)}, f32[2,2,5,5]{3,2,1,0:T(8,128)}, u32[]{:S(2)}) copy-start(f32[2,2,5,5]{3,2,1,0:T(8,128)} %copy.143) | copy-start | bytes 1204
  71.7 7.5 %copy-start.32 = (f32[2,2,5,5]{3,2,1,0:T(8,128)S(1)}, f32[2,2,5,5]{3,2,1,0:T(8,128)}, u32[]{:S(2)}) copy-start(f32[2,2,5,5]{3,2,1,0:T(8,128)} %copy.142) | copy-start | bytes 1204
  71.7 7.5 %copy-start.33 = (f32[2,2,5,5]{3,2,1,0:T(8,128)S(1)}, f32[2,2,5,5]{3,2,1,0:T(8,128)}, u32[]{:S(2)}) copy-start(f32[2,2,5,5]{3,2,1,0:T(8,128)} %copy.141) | copy-start | bytes 1204
  71.7 7.5 %copy-start.34 = (f32[2,2,5,5]{3,2,1,0:T(8,128)S(1)}, f32[2,2,5,5]{3,2,1,0:T(8,128)}, u32[]{:S(2)}) copy-start(f32[2,2,5,5]{3,2,1,0:T(8,128)} %copy.140) | copy-start | bytes 1204
  79.2 13.4 %copy-start.2 = (s32[2,2,5,5,64]{4,3,2,1,0:T(8,128)S(1)}, s32[2,2,5,5,64]{4,3,2,1,0:T(8,128)}, u32[]{:S(2)}) copy-start(s32[2,2,5,5,64]{4,3,2,1,0:T(8,128)} %get-tuple-element.84) | copy-start | bytes 76804
  79.2 13.4 %copy-start.3 = (s32[2,2,5,5,64]{4,3,2,1,0:T(8,128)S(1)}, s32[2,2,5,5,64]{4,3,2,1,0:T(8,128)}, u32[]{:S(2)}) copy-start(s32[2,2,5,5,64]{4,3,2,1,0:T(8,128)} %get-tuple-element.85) | copy-start | bytes 76804
  79.2 13.4 %copy-start.4 = (s32[2,2,5,5,64]{4,3,2,1,0:T(8,128)S(1)}, s32[2,2,5,5,64]{4,3,2,1,0:T(8,128)}, u32[]{:S(2)}) copy-start(s32[2,2,5,5,64]{4,3,2,1,0:T(8,128)} %get-tuple-element.86) | copy-start | bytes 76804
  79.2 13.4 %copy-start.5 = (s32[2,2,5,5,64]{4,3,2,1,0:T(8,128)S(1)}, s32[2,2,5,5,64]{4,3,2,1,0:T(8,128)}, u32[]{:S(2)}) copy-start(s32[2,2,5,5,64]{4,3,2,1,0:T(8,128)} %get-tuple-element.87) | copy-start | bytes 76804
  79.3 13.4 %copy-start.6 = (s32[2,2,5,5,64]{4,3,2,1,0:T(8,128)S(1)}, s32[2,2,5,5,64]{4,3,2,1,0:T(8,128)}, u32[]{:S(2)}) copy-start(s32[2,2,5,5,64]{4,3,2,1,0:T(8,128)} %get-tuple-element.88) | copy-start | bytes 76804
  79.3 13.4 %copy-start.7 = (s32[2,2,5,5,64]{4,3,2,1,0:T(8,128)S(1)}, s32[2,2,5,5,64]{4,3,2,1,0:T(8,128)}, u32[]{:S(2)}) copy-start(s32[2,2,5,5,64]{4,3,2,1,0:T(8,128)} %get-tuple-element.89) | copy-start | bytes 76804
  79.3 13.4 %copy-start.8 = (s32[2,2,5,5,64]{4,3,2,1,0:T(8,128)S(1)}, s32[2,2,5,5,64]{4,3,2,1,0:T(8,128)}, u32[]{:S(2)}) copy-start(s32[2,2,5,5,64]{4,3,2,1,0:T(8,128)} %get-tuple-element.90) | copy-start | bytes 76804
  79.3 13.4 %copy-start.9 = (s32[2,2,5,5,64]{4,3,2,1,0:T(8,128)S(1)}, s32[2,2,5,5,64]{4,3,2,1,0:T(8,128)}, u32[]{:S(2)}) copy-start(s32[2,2,5,5,64]{4,3,2,1,0:T(8,128)} %get-tuple-element.91) | copy-start | bytes 76804
  79.3 13.4 %copy-start.20 = (f32[2,2,5,5]{3,2,1,0:T(8,128)S(1)}, f32[2,2,5,5]{3,2,1,0:T(8,128)}, u32[]{:S(2)}) copy-start(f32[2,2,5,5]{3,2,1,0:T(8,128)} %copy.131) | copy-start | bytes 1204
  79.3 13.4 %copy-start.21 = (f32[2,2,5,5]{3,2,1,0:T(8,128)S(1)}, f32[2,2,5,5]{3,2,1,0:T(8,128)}, u32[]{:S(2)}) copy-start(f32[2,2,5,5]{3,2,1,0:T(8,128)} %copy.132) | copy-start | bytes 1204
  79.3 13.4 %copy-start.22 = (f32[2,2,5,5]{3,2,1,0:T(8,128)S(1)}, f32[2,2,5,5]{3,2,1,0:T(8,128)}, u32[]{:S(2)}) copy-start(f32[2,2,5,5]{3,2,1,0:T(8,128)} %copy.133) | copy-start | bytes 1204
  79.3 13.4 %copy-start.23 = (f32[2,2,5,5]{3,2,1,0:T(8,128)S(1)}, f32[2,2,5,5]{3,2,1,0:T(8,128)}, u32[]{:S(2)}) copy-start(f32[2,2,5,5]{3,2,1,0:T(8,128)} %copy.134) | copy-start | bytes 1204
  79.3 13.4 %copy-start.25 = (f32[2,2,5,5]{3,2,1,0:T(8,128)S(1)}, f32[2,2,5,5]{3,2,1,0:T(8,128)}, u32[]{:S(2)}) copy-start(f32[2,2,5,5]{3,2,1,0:T(8,128)} %copy.135) | copy-start | bytes 1204
  79.3 13.4 %copy-start.27 = (f32[2,2,5,5]{3,2,1,0:T(8,128)S(1)}, f32[2,2,5,5]{3,2,1,0:T(8,128)}, u32[]{:S(2)}) copy-start(f32[2,2,5,5]{3,2,1,0:T(8,128)} %copy.136) | copy-start | bytes 1204
  79.4 13.4 %copy-start.30 = (f32[2,2,5,5]{3,2,1,0:T(8,128)S(1)}, f32[2,2,5,5]{3,2,1,0:T(8,128)}, u32[]{:S(2)}) copy-start(f32[2,2,5,5]{3,2,1,0:T(8,128)} %copy.129) | copy-start | bytes 1204
  122.5 11.3 %copy-start.1 = (bf16[2,344,320]{1,2,0:T(8,128)(2,1)S(1)}, bf16[2,344,320]{1,2,0:T(8,128)(2,1)}, u32[]{:S(2)}) copy-start(bf16[2,344,320]{1,2,0:T(8,128)(2,1)} %dynamic-slice_bitcast_fusion) | copy-start | bytes 1320964
  122.5 278.2 %all-to-all-start = ((bf16[2,2,2,320,320]{4,2,1,0,3:T(2,128)(2,1)}), bf16[2,2,2,320,320]{4,2,1,0,3:T(2,128)(2,1)S(1)}, u32[]{:S(2)}, u32[]{:S(2)}) async-start(bf16[2,2,2,320,320]{4,2,1,0,3:T(2,128)(2,1)} %reshape.249), calls=%async_computation | async-start | bytes 3932160 | tf_op jit(solution)/shard_map/all_to_all | solution.py:151
  133.5 249.7 %all-reduce.3.cloned.1.call-start = ((), (), s32[]{:S(2)}) async-start(), calls=%async_computation.1 | async-start | bytes 5242880 | tf_op jit(solution)/shard_map/psum | solution.py:31
Sparse Core Ops, SparseCore 0:
  137.8 245.3 all-reduce.2
where the time goes:
time: 464 us; the launch traced here: 462 us
  waiting for transfers between devices  245 us (53%)
  local copies, waits for them, and re-layouts  107 us (23%)
  other arithmetic  43.7 us (9%)
  matrix products  27 us (6%)
  between operations  19.7 us (4%)
  starting transfers between devices  18.8 us (4%)
    psum x1, waiting for transfers between devices, spread(): return lax.psum(kept, axis)  245 us
    unnamed x91, local copies, waits for them, and re-layouts  20.8 us
    reshape x2, local copies, waits for them, and re-layouts, resample(): chips_out.transpose(0, 1, 2, 3, 5, 4, 6)  15.9 us
    dot_general x1, matrix products, resample(): jnp.einsum('dtcariv,dtarjv->dtcarij', partial_rows, across, preferred_ele...  13.8 us
    dot_general x1, matrix products, resample(): jnp.einsum('dtariw,dtcarwv->dtcariv', azimuth, windows, preferred_element...  13.2 us
    reduce_sum x4, other arithmetic, box_sum(): return jnp.sum(blocked, axis=(3, 5))  12.9 us
    all_to_all x1, starting transfers between devices, per_device(): lax.all_to_all(resampled, 'date', split_axis=3, concat_axis=0, tiled=True)  11 us
  transfers between devices with their start and end apart: 4, of which 1 were waited for; matrix products, arithmetic and copies ran while one was open for 10% of the time, Pallas kernels for 0%

commit v1 on v0

--- a/solution.py
+++ b/solution.py
@@ -11,6 +11,12 @@
 LOOK_RG = 20
 MARGIN = 12
 epsilon = 1e-06
+
+
+def add_all(value, axis):
+    parts = lax.all_gather(value, axis, axis=0, tiled=False)
+    acc = parts.sum(axis=0)
+    return acc
 
 
 def padded_2(block, sides, width):
@@ -28,7 +34,7 @@
 
 def spread(value, axis, source):
     kept = jnp.where(lax.axis_index(axis) == source, value, 0).astype(value.dtype)
-    return lax.psum(kept, axis)
+    return add_all(kept, axis)
 
 
 def sinc_matrix(shift_part, fraction_part):

time: 464 us -> 274 us (0.59)
  waiting for transfers between devices: 245 us -> 4.04 us
  blocking collectives: 0 us -> 68.7 us
  local copies, waits for them, and re-layouts: 107 us -> 86 us
  other arithmetic: 43.7 us -> 59.6 us
  starting transfers between devices: 18.8 us -> 7.65 us
    psum x1 -> x0, waiting for transfers between devices: 245 us -> none  [spread(): return lax.psum(kept, axis)]
    all_to_all x0 -> x1, blocking collectives: none -> 68.7 us  [per_device(): lax.all_to_all(resampled, 'date', split_axis=3, concat_axis=0, tiled=True)]
    reduce_sum x0 -> x2, other arithmetic: none -> 17.4 us  [add_all(): acc = parts.sum(axis=0)]
    all_to_all x1 -> x0, starting transfers between devices: 11 us -> none  [per_device(): lax.all_to_all(resampled, 'date', split_axis=3, concat_axis=0, tiled=True)]
    broadcast_in_dim x17, local copies, waits for them, and re-layouts: 9.06 us -> 0.08 us  [sinc_matrix(): jnp.where(in_rows == target, weights[..., tap_index][..., None, None], 0.0)]
    unnamed x91 -> x27, local copies, waits for them, and re-layouts: 20.8 us -> 15.5 us
  transfers between devices with their start and end apart: 4 -> 4, of which waited for: 1 -> 1; matrix products, arithmetic and copies ran while one was open for 10% -> 51% of each run, Pallas kernels for 0% -> 0%
where the time goes in v1:
time: 274 us; the launch traced here: 273 us
  local copies, waits for them, and re-layouts  86 us (31%)
  blocking collectives  68.7 us (25%)
  other arithmetic  59.6 us (22%)
  matrix products  26.8 us (10%)
  between operations  19.7 us (7%)
  starting transfers between devices  7.65 us (3%)
  waiting for transfers between devices  4.04 us (1%)
    all_to_all x1, blocking collectives, per_device(): lax.all_to_all(resampled, 'date', split_axis=3, concat_axis=0, tiled=True)  68.7 us
    reduce_sum x2, other arithmetic, add_all(): acc = parts.sum(axis=0)  17.4 us
    unnamed x27, local copies, waits for them, and re-layouts  15.5 us
    reshape x2, local copies, waits for them, and re-layouts, resample(): chips_out.transpose(0, 1, 2, 3, 5, 4, 6)  15.2 us
    dot_general x1, matrix products, resample(): jnp.einsum('dtcariv,dtarjv->dtcarij', partial_rows, across, preferred_ele...  13.8 us
    reduce_sum x4, other arithmetic, box_sum(): return jnp.sum(blocked, axis=(3, 5))  13.1 us
    dot_general x1, matrix products, resample(): jnp.einsum('dtariw,dtcarwv->dtcariv', azimuth, windows, preferred_element...  13 us
    add x1, other arithmetic, multilook_pairs(): cross_real = early_real * later_real + early_imag * later_imag  9.16 us
  transfers between devices with their start and end apart: 4, of which 1 were waited for; matrix products, arithmetic and copies ran while one was open for 51% of the time, Pallas kernels for 0%

profile of v1, /device:TPU:1, one launch (start us, length us, event | category | flops | bytes accessed | tf_op | source)
XLA Modules:
  0.0 272.5 jit_solution(8703010946431363026)
XLA Ops:
  9.8 2.7 fusion.118
  13.2 2.0 constant_dynamic-slice_fusion.1
  15.2 1.3 copy.96
  17.2 0.9 slice_select_fusion.1
  21.1 1.0 slice_select_fusion
  22.2 1.3 collective-permute-start.1
  23.5 6.3 %collective-permute-start = (bf16[2,2,2,344,12]{3,4,2,1,0:T(8,128)(2,1)S(1)}, bf16[2,2,2,344,12]{3,4,2,1,0:T(8,128)(2,1)S(1)}, u32[]{:S(2)}, u32[]{:S(2)}) collective-permute-start(bf16[2,2,2,344,12]{3,4,2,1,0:T(8,128)(2,1)S(1)} %get-tuple-element.21), channel_id=1, source_target_pairs={{0,1},{1,2},{2,3},{3,4},{4,5},{5,6},{6,7},{8,9},{9,10},{10,11},{11... | collective-permute-start | bytes 198152 | tf_op jit(solution)/shard_map/ppermute | solution.py:27
  29.9 3.2 %fusion.114 = (f32[2,2,5,5]{3,1,2,0:T(2,128)S(1)}, f32[2,2,5,5]{3,1,2,0:T(2,128)S(1)}) fusion(f32[2,2,5,5]{3,1,2,0:T(2,128)S(1)} %get-tuple-element.45, f32[8]{0:T(128)S(1)} %convert_add_fusion, f32[2,2,5,5]{3,1,2,0:T(2,128)S(1)} %get-tuple-element.44), kind=kLoop, calls=%fused_computation.182 | loop fusion | flops 62200 | bytes 1632 | tf_op jit(solution)/shard_map/reduce_sum | solution.py:46
  33.0 3.1 %broadcast_divide_fusion.1 = (f32[2,2,5,5,8]{3,1,2,0,4:T(2,128)S(1)}, f32[2,2,5,5,8]{3,1,2,0,4:T(2,128)S(1)}) fusion(f32[2,2,5,5]{3,1,2,0:T(2,128)S(1)} %get-tuple-element.10, f32[2,2,5,5]{3,1,2,0:T(2,128)S(1)} %get-tuple-element.45, f32[8]{0:T(128)S(1)} %convert_add_fusion, f32[2,2,5,5]{3,1,2,0:T(2,128)S(1)} %get-tuple-element.11, ...), kind=kLoop, calls=%fused_computation.180 | loop fusion | flops 62400 | bytes 8032 | tf_op jit(solution)/shard_map/div | solution.py:46
  36.9 0.7 fusion.72
  37.7 0.7 bitcast_dynamic-update-slice_fusion.14
  40.6 0.8 fusion.70
  41.4 0.8 bitcast_dynamic-update-slice_fusion.11
  42.3 0.8 bitcast_dynamic-update-slice_fusion.10
  43.1 0.8 bitcast_dynamic-update-slice_fusion.9
  43.9 0.8 fusion.69
  48.4 0.9 fusion.66
  49.2 0.9 bitcast_dynamic-update-slice_fusion.5
  50.1 0.8 bitcast_dynamic-update-slice_fusion.4
  50.9 0.8 bitcast_dynamic-update-slice_fusion.3
  51.7 0.8 fusion.65
  52.6 0.7 fusion.64
  54.0 0.7 bitcast_dynamic-update-slice_fusion.1
  56.2 7.2 %copy.113 = bf16[2,2,2,25,88,88]{5,4,2,3,1,0:T(8,128)(2,1)} copy(bf16[2,2,2,25,88,88]{4,5,2,1,0,3:T(8,128)(2,1)} %fusion.62) | data formatting | bytes 6195200 | tf_op jit(solution)/shard_map/stack | solution.py:120
  63.4 13.0 %fusion.4.clone.5 = bf16[2,2,2,5,5,64,88]{6,5,2,4,3,1,0:T(8,128)(2,1)S(1)} fusion(bf16[2,2,2,5,5,88,88]{6,5,2,4,3,1,0:T(8,128)(2,1)} %bitcast.222, f32[2,2,5,5]{3,2,1,0:T(8,128)S(1)} %copy.122, s32[2,2,5,5,64]{4,3,2,1,0:T(8,128)S(1)} %get-tuple-element.55, f32[2,2,5,5]{3,2,1,0:T(8,128)S(1)} %copy.121, ...), kind=kOutput, calls=%fused_computation.3.clone.clone.clone.clone.clone.2 | convolution fusion | flops 212889600 | bytes 5558400 | tf_op jit(solution)/shard_map/dtariw,dtcarwv->dtcariv/dot_general | solution.py:125
  76.4 13.8 %fusion.122 = (f32[2,2,2,5,64,5,64]{4,6,2,5,3,1,0:T(8,128)}, bf16[2,2,2,5,64,5,64]{4,6,2,5,3,1,0:T(8,128)(2,1)}) fusion(f32[2,2,5,5]{3,2,1,0:T(8,128)S(1)} %copy.112, s32[2,2,5,5,64]{4,3,2,1,0:T(8,128)S(1)} %get-tuple-element.88, f32[2,2,5,5]{3,2,1,0:T(8,128)S(1)} %copy.111, s32[2,2,5,5,64]{4,3,2,1,0:T(8,128)S(1)} %get-tuple-element.87, ...), kind=kOutput, calls=%fused_computation.226 | convolution fusion | flops 159334400 | bytes 7376000 | tf_op jit(solution)/shard_map/dtcariv,dtarjv->dtcarij/dot_general | solution.py:128
  90.2 8.0 %copy.141 = bf16[2,2,2,5,64,5,64]{6,5,2,1,0,4,3:T(8,128)(2,1)} copy(bf16[2,2,2,5,64,5,64]{4,6,2,5,3,1,0:T(8,128)(2,1)} %get-tuple-element.71) | data formatting | bytes 3276800 | tf_op jit(solution)/shard_map/reshape | solution.py:131
  98.2 7.2 %reshape.251 = bf16[2,2,2,320,320]{4,2,1,0,3:T(2,128)(2,1)S(1)} reshape(bf16[2,2,2,5,64,5,64]{6,5,2,1,0,4,3:T(8,128)(2,1)} %copy.141) | data formatting | bytes 3276800 | tf_op jit(solution)/shard_map/reshape | solution.py:131
  105.4 68.7 %all_to_all.4 = bf16[2,2,2,320,320]{4,2,1,0,3:T(2,128)(2,1)S(1)} all-to-all(bf16[2,2,2,320,320]{4,2,1,0,3:T(2,128)(2,1)S(1)} %reshape.251), channel_id=1, replica_groups=mesh['date'=32,'strip'=8] {'date'}, dimensions={3} | all-to-all | bytes 3276800 | tf_op jit(solution)/shard_map/all_to_all | solution.py:157
  174.4 3.0 %copy.132 = f32[2,2,2,320,320]{4,2,3,1,0:T(2,128)S(1)} copy(f32[2,2,2,320,320]{4,3,2,1,0:T(8,128)S(1)} %copy_convert_fusion) | data formatting | bytes 6553600 | tf_op jit(solution)/shard_map/convert_element_type | solution.py:82
  177.4 1.3 copy.133
  178.8 9.2 %multiply_add_fusion.2 = (f32[63,2,1,10,320]{4,2,3,1,0:T(1,128)}, f32[63,2,1,10,320]{4,2,3,1,0:T(1,128)}, f32[63,2,1,10,320]{4,2,3,1,0:T(1,128)}, f32[63,2,1,10,320]{4,2,3,1,0:T(1,128)S(1)}) fusion(f32[64,2,2,10,320]{4,2,3,1,0:T(2,128)S(1)} %bitcast.214), kind=kLoop, calls=%fused_computation.35 | loop fusion | flops 4838400 | bytes 12902400 | tf_op jit(solution)/shard_map/add | solution.py:89
  187.9 7.4 %copy.134 = f32[63,2,1,10,320]{0,1,4,3,2:T(2,128)} copy(f32[63,2,1,10,320]{4,2,3,1,0:T(1,128)} %get-tuple-element.14) | data formatting | bytes 3225600 | tf_op jit(solution)/shard_map/add | solution.py:89
  195.4 7.5 %copy.135 = f32[63,2,1,10,320]{0,1,4,3,2:T(2,128)} copy(f32[63,2,1,10,320]{4,2,3,1,0:T(1,128)} %get-tuple-element.15) | data formatting | bytes 3225600 | tf_op jit(solution)/shard_map/add | solution.py:91
  202.8 3.3 %reduce_sum.128 = f32[63,2,2,16]{0,1,3,2:T(2,128)S(1)} reduce(f32[63,2,2,5,16,20]{0,1,5,4,3,2:T(2,128)} %bitcast.218, f32[]{:T(128)} %constant.100.clone.1), dimensions={3,5}, to_apply=%region_8.10 | reduce | flops 399168 | bytes 1628932 | tf_op jit(solution)/shard_map/reduce_sum | solution.py:99
  206.1 3.3 %reduce_sum.129 = f32[63,2,2,16]{0,1,3,2:T(2,128)S(1)} reduce(f32[63,2,2,5,16,20]{0,1,5,4,3,2:T(2,128)} %bitcast.219, f32[]{:T(128)} %constant.100.clone.1), dimensions={3,5}, to_apply=%region_9.11 | reduce | flops 399168 | bytes 1628932 | tf_op jit(solution)/shard_map/reduce_sum | solution.py:99
  209.4 7.4 %copy.136 = f32[63,2,1,10,320]{0,1,4,3,2:T(2,128)} copy(f32[63,2,1,10,320]{4,2,3,1,0:T(1,128)} %get-tuple-element.16) | data formatting | bytes 3225600 | tf_op jit(solution)/shard_map/add | solution.py:92
  216.8 3.2 %reduce_sum.130 = f32[63,2,2,16]{0,1,3,2:T(2,128)S(1)} reduce(f32[63,2,2,5,16,20]{0,1,5,4,3,2:T(2,128)} %bitcast.221, f32[]{:T(128)} %constant.100.clone.1), dimensions={3,5}, to_apply=%region_10.12 | reduce | flops 399168 | bytes 1628932 | tf_op jit(solution)/shard_map/reduce_sum | solution.py:99
  220.1 4.9 %copy.137 = f32[63,2,1,10,320]{0,1,4,3,2:T(2,128)} copy(f32[63,2,1,10,320]{4,2,3,1,0:T(1,128)S(1)} %get-tuple-element.17) | data formatting | bytes 3225600 | tf_op jit(solution)/shard_map/sub | solution.py:90
  225.0 3.3 %reduce_sum.131 = f32[63,2,2,16]{0,1,3,2:T(2,128)S(1)} reduce(f32[63,2,2,5,16,20]{0,1,5,4,3,2:T(2,128)} %bitcast.220, f32[]{:T(128)} %constant.100.clone.1), dimensions={3,5}, to_apply=%region_11.13 | reduce | flops 399168 | bytes 1628932 | tf_op jit(solution)/shard_map/reduce_sum | solution.py:99
  229.0 8.8 %reduce_sum.118 = bf16[2,320,320]{2,1,0:T(8,128)(2,1)S(1)} reduce(bf16[32,2,320,320]{3,2,1,0:T(8,128)(2,1)} %bitcast.215, bf16[]{:T(256)} %constant.94.clone.1), dimensions={0}, to_apply=%region_0.1 | reduce | flops 6348800 | bytes 13516802 | tf_op jit(solution)/shard_map/reduce_sum | solution.py:18
  237.8 4.0 %all-gather.7.cloned.1.call-done = bf16[64,320,320]{2,1,0:T(8,128)(2,1)} async-done(((bf16[2,320,320]{2,1,0:T(8,128)(2,1)}), bf16[64,320,320]{2,1,0:T(8,128)(2,1)}) %all-gather.7.cloned.1.call-update) | async-done | bytes 13107216 | tf_op jit(solution)/shard_map/all_gather | solution.py:17
  241.8 8.6 %reduce_sum.119 = bf16[2,320,320]{2,1,0:T(8,128)(2,1)S(1)} reduce(bf16[32,2,320,320]{3,2,1,0:T(8,128)(2,1)} %bitcast.216, bf16[]{:T(256)} %constant.94.clone.1), dimensions={0}, to_apply=%region_1.2 | reduce | flops 6348800 | bytes 13516802 | tf_op jit(solution)/shard_map/reduce_sum | solution.py:18
  251.4 0.9 maximum_convert_fusion
  252.9 2.8 %slice_bitcast_fusion.3 = (f32[2,5,64,5,64]{4,3,2,1,0:T(8,128)}, f32[2,5,64,5,64]{4,3,2,1,0:T(8,128)}) fusion(f32[2,2,5,64,5,64]{5,4,3,2,1,0:T(8,128)S(1)} %maximum_convert_fusion), kind=kLoop, calls=%fused_computation.28 | loop fusion | bytes 3276800 | tf_op jit(solution)/shard_map/mul | solution.py:73
  255.7 2.0 copy.103
  257.7 2.9 %copy.124 = f32[2,5,64,5,64]{2,4,3,1,0:T(8,128)} copy(f32[2,5,64,5,64]{4,3,2,1,0:T(8,128)} %get-tuple-element.13) | data formatting | bytes 1638400 | tf_op jit(solution)/shard_map/mul | solution.py:73
  260.6 4.4 %add_reduce_fusion.1 = (f32[2,2,5,5]{3,2,1,0:T(8,128)S(1)}, f32[2,2,5,5]{3,2,1,0:T(8,128)S(1)}, f32[2,2,5,5]{3,2,1,0:T(8,128)S(1)}) fusion(f32[2,2,2,5,64,5,64]{4,6,2,5,3,1,0:T(8,128)} %get-tuple-element.70, f32[2,5,64,5,64]{2,4,3,1,0:T(8,128)} %copy.124, f32[2,5,64,5,64]{2,4,3,1,0:T(8,128)S(1)} %copy.103), kind=kLoop, calls=%fused_computation.6 | loop fusion | flops 4914900 | bytes 4916400 | tf_op jit(solution)/shard_map/reduce_sum | solution.py:73
  (66 shorter events, 13.6 us)
Async XLA Ops:
  7.2 221.8 %all-gather.5.cloned.1.call-start = ((), (), s32[]{:S(2)}) async-start(), calls=%async_computation.1 | async-start | bytes 16220160 | tf_op jit(solution)/shard_map/all_gather | solution.py:17
  13.2 8.9 %copy-start = (bf16[2,2,2,344,320]{3,4,2,1,0:T(8,128)(2,1)S(1)}, bf16[2,2,2,344,320]{3,4,2,1,0:T(8,128)(2,1)}, u32[]{:S(2)}) copy-start(bf16[2,2,2,344,320]{3,4,2,1,0:T(8,128)(2,1)} %param.5) | copy-start | bytes 5283844
  15.2 14.6 %copy-start.1 = (s32[2,2,2,5,5]{4,2,3,1,0:T(2,128)S(1)}, s32[2,2,2,5,5]{4,2,3,1,0:T(2,128)}, u32[]{:S(2)}) copy-start(s32[2,2,2,5,5]{4,2,3,1,0:T(2,128)} %param.6) | copy-start | bytes 2404
  15.2 14.6 %copy-start.2 = (s32[2,2,2,5,5]{4,2,3,1,0:T(2,128)S(1)}, s32[2,2,2,5,5]{4,2,3,1,0:T(2,128)}, u32[]{:S(2)}) copy-start(s32[2,2,2,5,5]{4,2,3,1,0:T(2,128)} %param.7) | copy-start | bytes 2404
  18.2 223.6 %all-gather.7.cloned.1.call-start = ((), (), s32[]{:S(2)}) async-start(), calls=%async_computation.2 | async-start | bytes 16220160 | tf_op jit(solution)/shard_map/all_gather | solution.py:17
  22.2 14.7 %collective-permute-start.1 = (bf16[2,2,2,344,12]{3,4,2,1,0:T(8,128)(2,1)S(1)}, bf16[2,2,2,344,12]{3,4,2,1,0:T(8,128)(2,1)S(1)}, u32[]{:S(2)}, u32[]{:S(2)}) collective-permute-start(bf16[2,2,2,344,12]{3,4,2,1,0:T(8,128)(2,1)S(1)} %get-tuple-element.20), channel_id=1, source_target_pairs={{1,0},{2,1},{3,2},{4,3},{5,4},{6,5},{7,6},{9,8},{10,9},{11,10},{12... | collective-permute-start | bytes 198152 | tf_op jit(solution)/shard_map/ppermute | solution.py:30
  23.5 13.5 %collective-permute-start = (bf16[2,2,2,344,12]{3,4,2,1,0:T(8,128)(2,1)S(1)}, bf16[2,2,2,344,12]{3,4,2,1,0:T(8,128)(2,1)S(1)}, u32[]{:S(2)}, u32[]{:S(2)}) collective-permute-start(bf16[2,2,2,344,12]{3,4,2,1,0:T(8,128)(2,1)S(1)} %get-tuple-element.21), channel_id=1, source_target_pairs={{0,1},{1,2},{2,3},{3,4},{4,5},{5,6},{6,7},{8,9},{9,10},{10,11},{11... | collective-permute-start | bytes 198152 | tf_op jit(solution)/shard_map/ppermute | solution.py:27
Sparse Core Ops, SparseCore 0:
  18.3 98.7 all-gather.4
  118.9 122.8 all-gather.6
